TPU v7x, 128 devices: a whole 4x4x4 slice. The times are simulated.
128 devices in a mesh: box: 32 (over x, z, core), dir: 4 (over y).
Axes of the slice: x: 4, y: 4, z: 4, core: 2. Of those that a mesh axis runs over, the one named last changes fastest.
Arguments:
- child_pat: bfloat16 [4096, 2, 8, 2048], P('box', None, None, 'dir'), may hold values from -6 to 6
- interp: bfloat16 [64, 4, 128, 128], P('dir'), may hold values from -0.25 to 0.25
- interp_blocks: int32 [64, 4], P('dir'), may hold values from 0 to 15, as said below
- shift_angle: float32 [8, 8192], P(None, 'dir'), may hold values from -3.140625 to 3.140625
- slot_parent: int32 [512], replicated, may hold values from 0 to 511, each once
- far_list: int32 [512, 189], replicated, may hold values from -1 to 511, as said below
- trans: float32 [2, 343, 8192], P(None, None, 'dir'), may hold values from -0.15625 to 0.15625
Outputs:
- far_field: float32 [512, 2, 8, 8192], P('box', None, None, 'dir')
Inputs may be any that keep to these rules, and one draw needn't show every extreme that they name: `interp_blocks`: entry (j, b) is (j * 16 // 64 + o) modulo 16, for four different o of -2 to 2 in increasing order. `far_list`: row p lists, in increasing order of code(p, q), the occupied parents q whose own parents are neighbours of p's parent (coordinates differ by at most one) and that are not neighbours of p, then -1 to the end; each coordinate of q - p lies within -3 to 3; some row lists 189 partners.
All inputs are finite; a program needn't handle non-finite values.
Results may differ from a plain program's by a relative error of at most 0.0029.
Values may be sent and summed in bfloat16 or wider, within the bound.
A program may use at most 192 MiB of HBM per device.

v0:
```python
import jax
import jax.numpy as jnp
from jax import lax
from jax.experimental import pallas as pl
from jax.experimental.pallas import tpu as pltpu
from jax.sharding import PartitionSpec as P

G = 8
F1 = 18
NF = F1 * F1


def toom_in(v):
    a, b = v[0] + v[2], v[1] + v[3]
    c, d = v[0] + 4.0 * v[2], 2.0 * v[1] + 8.0 * v[3]
    return [v[0], v[3], a + b, a - b, c + d, c - d]


def line_in(x):
    even, odd = x[0::2], x[1::2]
    both = [e + o for e, o in zip(even, odd)]
    return toom_in(both) + toom_in(odd) + toom_in(even)


def toom_kernel(k):
    h2, h1, h0 = k
    a, b = (h0 + h2) * 0.5, h1 * 0.5
    c, d = (h0 + 4.0 * h2) * (1.0 / 24.0), h1 * (1.0 / 12.0)
    return [h0, h2, a + b, a - b, c + d, c - d]


def line_kernel(t):
    k0 = [t[1], t[3], t[5]]
    up = [t[2] - t[1], t[4] - t[3], t[6] - t[5]]
    down = [t[0] - t[1], t[2] - t[3], t[4] - t[5]]
    return toom_kernel(k0) + toom_kernel(up) + toom_kernel(down)


def toom_out(m):
    z0, z5 = m[0], m[1]
    e1, o1 = m[2] + m[3], m[2] - m[3]
    e2, d2 = m[4] + m[5], m[4] - m[5]
    z4 = e2 - e1 * (1.0 / 3.0) + z0 * 0.25
    z2 = e1 - z0 - z4
    z3 = 2.0 * d2 - o1 * (1.0 / 3.0) - 5.0 * z5
    z1 = o1 - z3 - z5
    return [z1, z2, z3, z4]


def line_out(m):
    base, up, down = toom_out(m[0:6]), toom_out(m[6:12]), toom_out(m[12:18])
    out = []
    for i in range(4):
        out += [base[i] + up[i], base[i] + down[i]]
    return out


TURNS = [(1, 1), (3, 1), (3, 3), (1, 3), (2, 2), (1, 2), (2, 1), (3, 2), (2, 3), (1, 0), (0, 1), (3, 0), (0, 3), (2, 0), (0, 2)]
PEERS = [(0, 0, 1)] + [(x, z, c) for c in range(2) for x, z in TURNS]
CHUNKS = 8


def peers_of(bb):
    x, z, c = bb // 8, (bb // 2) % 4, bb % 2
    return [((x + dx) % 4) * 8 + ((z + dz) % 4) * 2 + (c + dc) % 2 for dx, dz, dc in PEERS]


def main_kernel(
    child, interp, blocks_in, angle_in, slot_in, far, trans, out,
    own, before, after, weights, weight, total, stage, cosine, sine, raw, tab_z, tab, tiles,
    listed, occ, mask, slot_vec, slot_of, blocks, angle, slot_parent,
    pats, wide_x, later, grid_x, lines, spec, back,
    load_sem, halo_send, halo_recv, move_send, move_recv, local_sem, home_sem, back_send, back_recv,
):
    bb, dd = lax.axis_index("box"), lax.axis_index("dir")
    dirs = lax.axis_size("dir")
    rows = 2048 // CHUNKS
    peers = peers_of(bb)
    above, below = (dd + 1) % dirs, (dd + dirs - 1) % dirs
    barrier = pltpu.get_barrier_semaphore()
    pl.semaphore_signal(barrier, 1, device_id={"dir": above})
    pl.semaphore_signal(barrier, 1, device_id={"dir": below})
    for peer in peers:
        pl.semaphore_signal(barrier, 1, device_id={"box": peer})
    first = pl.multiple_of((bb // 2) * 128, 128)
    loads = [
        pltpu.make_async_copy(trans.at[:, :, pl.ds(first, 128)], raw, load_sem.at[0]),
        pltpu.make_async_copy(interp, weights, load_sem.at[1]),
        pltpu.make_async_copy(child, own, load_sem.at[2]),
        pltpu.make_async_copy(far, listed, load_sem.at[3]),
        pltpu.make_async_copy(blocks_in, blocks, load_sem.at[4]),
        pltpu.make_async_copy(slot_in, slot_parent, load_sem.at[5]),
        pltpu.make_async_copy(angle_in, angle, load_sem.at[6]),
    ]
    for copy in loads:
        copy.start()
    pl.semaphore_wait(barrier, len(peers) + 2)

    def halo(i):
        at = pl.ds(pl.multiple_of(i * rows, rows), rows)
        return [
            pltpu.make_async_remote_copy(
                child.at[at, pl.ds(256, 256)], before.at[at, :],
                halo_send.at[0, i], halo_recv.at[0, i], device_id={"dir": above},
            ),
            pltpu.make_async_remote_copy(
                child.at[at, pl.ds(0, 256)], after.at[at, :],
                halo_send.at[1, i], halo_recv.at[1, i], device_id={"dir": below},
            ),
        ]

    for i in range(CHUNKS):
        for copy in halo(i):
            copy.start()

    loads[6].wait()
    cosine[...] = jnp.cos(angle[...])
    sine[...] = jnp.sin(angle[...])
    loads[1].wait()
    loads[4].wait()
    for j in range(16):
        rel = [(blocks[b, j] - (dd * 4 + j // 4) + 18) & 15 for b in range(4)]
        for o in range(5):
            value = None
            for b in (o - 1, o):
                if 0 <= b < 4:
                    term = weights[j, b].astype(jnp.float32) * jnp.where(rel[b] == o, 1.0, 0.0)
                    value = term if value is None else value + term
            lanes = pl.ds((j % 4) * 128, 128)
            weight[j // 4, pl.ds(o * 128, 128), lanes] = value.astype(jnp.bfloat16)

    loads[3].wait()
    loads[5].wait()
    lane = lax.broadcasted_iota(jnp.int32, (189, 128), 1)
    for t in range(4):
        watch = listed[:, pl.ds((t + 1 if t < 3 else 2) * 128, 128)]
        occ[t : t + 1, :] = jnp.max(jnp.where(watch == lane + t * 128, 1.0, 0.0), axis=0, keepdims=True)
    ident = lax.broadcasted_iota(jnp.int32, (4, 128), 0) * 128 + lax.broadcasted_iota(jnp.int32, (4, 128), 1)
    for s in range(16):
        held = jnp.where(ident == slot_parent[bb * 16 + s], occ[...], 0.0)
        held = jnp.max(jnp.max(held, axis=1, keepdims=True), axis=0, keepdims=True)
        mask[s] = jnp.broadcast_to(held, (8, 128))

    def invert(i, found):
        return tuple(
            jnp.where(ident == slot_parent[i * 4 + k], i * 4 + k, found[k]) for k in range(4)
        )

    zero = jnp.zeros((4, 128), jnp.int32)
    found = lax.fori_loop(0, 128, invert, (zero,) * 4, unroll=4)
    slot_vec[...] = jnp.maximum(jnp.maximum(found[0], found[1]), jnp.maximum(found[2], found[3]))
    to_scalar = [
        pltpu.make_async_copy(slot_vec.at[t], slot_of.at[pl.ds(t * 128, 128)], load_sem.at[7 + t])
        for t in range(4)
    ]
    for copy in to_scalar:
        copy.start()

    loads[0].wait()
    for x in range(2, 5):
        for y in range(2, 5):
            for z in range(2, 5):
                raw[x * 49 + y * 7 + z] = jnp.zeros((2, 128), jnp.float32)

    def table_x(i, carry):
        t = [raw[x * 49 + i] for x in range(7)]
        vals = [t[1], t[3], t[5], t[2] - t[1], t[4] - t[3], t[6] - t[5]]
        vals += [t[0] - t[1], t[2] - t[3], t[4] - t[5]]
        for g, v in enumerate(vals):
            tab[i, g] = v
        return carry

    lax.fori_loop(0, 49, table_x, 0)

    def table_z(y, carry):
        def inner(g, carry):
            vals = line_kernel([tab[y * 7 + z, g] for z in range(7)])
            for fz, v in enumerate(vals):
                tab_z[y * F1 + fz, g] = v
            return carry

        return lax.fori_loop(0, 9, inner, carry, unroll=3)

    lax.fori_loop(0, 7, table_z, 0)

    def table_y(fz, carry):
        def inner(g, carry):
            vals = line_kernel([tab_z[y * F1 + fz, g] for y in range(7)])
            for fy, v in enumerate(vals):
                tab[fy * F1 + fz, g] = v
            return carry

        return lax.fori_loop(0, 9, inner, carry, unroll=3)

    lax.fori_loop(0, F1, table_y, 0)
    loads[2].wait()
    row = lax.broadcasted_iota(jnp.int32, (8, 128), 0)
    low = row < 4

    def chunk(i, carry):
        for copy in halo(i):
            copy.wait_recv()
        at = pl.ds(pl.multiple_of(i * rows, rows), rows)
        for c in range(4):
            parts = []
            if c < 2:
                parts.append((before, c * 128, (2 - c) * 128, 0))
            lo, hi = max(c, 2), min(c + 5, 6)
            parts.append((own, (lo - 2) * 128, (hi - lo) * 128, (lo - c) * 128))
            if c > 1:
                parts.append((after, 0, (c - 1) * 128, (6 - c) * 128))
            acc = None
            for ref, col, width, wrow in parts:
                piece = jnp.dot(
                    ref[at, pl.ds(col, width)],
                    weight[c, pl.ds(wrow, width), :],
                    preferred_element_type=jnp.float32,
                )
                acc = piece if acc is None else acc + piece
            total[...] = acc

            def tile_of(tile, carry, c=c):
                lane = pl.multiple_of(tile * 128, 128)
                wide = pl.multiple_of(c * 512 + tile * 128, 128)
                halves = [[], []]
                for k in range(2):
                    re = im = None
                    for h in range(8):
                        base = k * 128 + h * 16
                        ur = total[pl.ds(base, 8), pl.ds(lane, 128)]
                        ui = total[pl.ds(base + 8, 8), pl.ds(lane, 128)]
                        cs = jnp.broadcast_to(cosine[h : h + 1, pl.ds(wide, 128)], (8, 128))
                        sn = jnp.broadcast_to(sine[h : h + 1, pl.ds(wide, 128)], (8, 128))
                        r, m = cs * ur - sn * ui, sn * ur + cs * ui
                        re = r if re is None else re + r
                        im = m if im is None else im + m
                    keep = mask[2 * i + k]
                    re, im = re * keep, im * keep
                    halves[0].append(jnp.where(low, re, pltpu.roll(im, 4, 0)))
                    halves[1].append(jnp.where(low, pltpu.roll(re, 4, 0), im))
                for k in range(2):
                    value = jnp.concatenate(halves[k], axis=0).astype(jnp.bfloat16)
                    stage[(c * 4 + tile) * 2 + k, i] = value
                return carry

            lax.fori_loop(0, 4, tile_of, 0)
        for peer in peers:
            pltpu.make_async_remote_copy(
                stage.at[peer, i], pats.at[bb * 8 + i], move_send, move_recv,
                device_id={"box": peer},
            ).start()
        return carry

    lax.fori_loop(0, CHUNKS, chunk, 0)
    mine = pltpu.make_async_copy(stage.at[bb], pats.at[pl.ds(bb * 8, 8)], local_sem)
    mine.start()
    pick = (row & 2) == 0

    def expand(fy, carry):
        def inner(fz, carry):
            for g in range(9):
                here, there = tab.at[fy * F1 + fz, g], tab.at[fy * F1 + fz + 9, g]
                two = []
                for part in range(2):
                    left = jnp.broadcast_to(here[part : part + 1, :], (8, 128))
                    right = jnp.broadcast_to(there[part : part + 1, :], (8, 128))
                    two.append(jnp.where(pick, left, right))
                tiles[fy * 9 + fz, g, 0] = two[0]
                tiles[fy * 9 + fz, g, 1] = jnp.where(low, -two[1], two[1])
            return carry

        return lax.fori_loop(0, 9, inner, carry)

    lax.fori_loop(0, F1, expand, 0)
    for copy in to_scalar:
        copy.wait()
    mine.wait()
    pltpu.make_async_copy(pats.at[pl.ds(0, 248)], pats.at[pl.ds(0, 248)], move_recv).wait()

    def widen(i, carry):
        both = pats[i].astype(jnp.float32)
        wide_x[2 * i] = both[0:8]
        wide_x[2 * i + 1] = both[8:16]
        return carry

    lax.fori_loop(0, 256, widen, 0, unroll=8)

    for half in range(2):

        def in_z(i, carry):
            vals = []
            for z in range(8):
                at = i * 8 + z
                if half == 0:
                    left, right = wide_x[slot_of[at]], wide_x[slot_of[at + 256]]
                    vals.append(jnp.where(pick, left, pltpu.roll(right, 2, 0)))
                    later[at] = jnp.where(pick, pltpu.roll(left, 6, 0), right)
                else:
                    vals.append(later[at])
            for f, v in enumerate(line_in(vals)):
                lines[i * F1 + f] = v
            return carry

        lax.fori_loop(0, 32, in_z, 0, unroll=4)

        def in_y(x, carry):
            def inner(fz, carry):
                vals = line_in([lines[(x * 8 + y) * F1 + fz] for y in range(8)])
                for fy, v in enumerate(vals):
                    spec[fy * F1 + fz, x] = v
                return carry

            return lax.fori_loop(0, F1, inner, carry, unroll=3)

        lax.fori_loop(0, 4, in_y, 0)

        def product(fy, carry):
            def inner(fz, carry):
                here, there = fy * F1 + fz, fy * F1 + fz + 9
                src = [None] * 8
                for x in range(4):
                    left, right = spec[here, x], spec[there, x]
                    src[x] = jnp.where(pick, left, pltpu.roll(right, 2, 0))
                    src[x + 4] = jnp.where(pick, pltpu.roll(left, 6, 0), right)
                turn = [pltpu.roll(v, 4, 0) for v in src]
                sets = [
                    ([src[2 * j] + src[2 * j + 1] for j in range(4)], [turn[2 * j] + turn[2 * j + 1] for j in range(4)]),
                    (src[1::2], turn[1::2]),
                    (src[0::2], turn[0::2]),
                ]
                sums = []
                for g, (x, t) in enumerate(sets):
                    acc = [None] * 4
                    for j in range(-1, 2):
                        a = tiles[fy * 9 + fz, g * 3 + j + 1, 0]
                        b = tiles[fy * 9 + fz, g * 3 + j + 1, 1]
                        for i in range(4):
                            if 0 <= i + j < 4:
                                v = a * x[i + j] + b * t[i + j]
                                acc[i] = v if acc[i] is None else acc[i] + v
                    sums.append(acc)
                res = []
                for i in range(4):
                    res += [sums[0][i] + sums[1][i], sums[0][i] + sums[2][i]]
                for x in range(4):
                    spec[here, x] = jnp.where(pick, res[x], pltpu.roll(res[x + 4], 2, 0))
                    spec[there, x] = jnp.where(pick, pltpu.roll(res[x], 6, 0), res[x + 4])
                return carry

            return lax.fori_loop(0, 9, inner, carry, unroll=9)

        lax.fori_loop(0, F1, product, 0)

        def out_y(x, carry):
            def inner(fz, carry):
                vals = line_out([spec[fy * F1 + fz, x] for fy in range(F1)])
                for y, v in enumerate(vals):
                    lines[(x * 8 + y) * F1 + fz] = v
                return carry

            return lax.fori_loop(0, F1, inner, carry, unroll=3)

        lax.fori_loop(0, 4, out_y, 0)

        def out_z(i, carry):
            for z, v in enumerate(line_out([lines[i * F1 + f] for f in range(F1)])):
                grid_x[i * 8 + z] = v
                grid_x[256 + i * 8 + z] = pltpu.roll(v, 6, 0)
            return carry

        lax.fori_loop(0, 32, out_z, 0, unroll=4)

        def give(target, half=half):
            for q in range(4):
                vals = [grid_x[slot_parent[target * 16 + 4 * q + k]] for k in range(4)]
                pairs = [jnp.where(pick, vals[k], pltpu.roll(vals[k + 1], 2, 0)) for k in (0, 2)]
                back[half, target, q] = jnp.concatenate(pairs, axis=0).astype(jnp.bfloat16)

        for peer in peers:
            give(peer)
            pltpu.make_async_remote_copy(
                back.at[half, peer], out.at[half, bb], back_send.at[half], back_recv.at[half],
                device_id={"box": peer},
            ).start()
        give(bb)
        pltpu.make_async_copy(back.at[half, bb], out.at[half, bb], home_sem.at[half]).start()

    for i in range(CHUNKS):
        for copy in halo(i):
            copy.wait_send()
    most = pl.ds(0, 31)
    pltpu.make_async_copy(stage.at[most], stage.at[most], move_send).wait()
    for half in range(2):
        pltpu.make_async_copy(back.at[half, bb], out.at[half, bb], home_sem.at[half]).wait()
        sent, got = back.at[half, most], out.at[half, most]
        pltpu.make_async_copy(sent, sent, back_send.at[half]).wait()
        pltpu.make_async_copy(got, got, back_recv.at[half]).wait()


def far_pieces(child, interp, blocks, angle, slot_parent, far, trans):
    any_space = pl.BlockSpec(memory_space=pl.ANY)
    return pl.pallas_call(
        main_kernel,
        in_specs=[any_space] * 7,
        out_specs=any_space,
        out_shape=jax.ShapeDtypeStruct((2, 32, 4, 16, 128), jnp.bfloat16),
        scratch_shapes=[
            pltpu.VMEM((2048, 512), jnp.bfloat16),
            pltpu.VMEM((2048, 256), jnp.bfloat16),
            pltpu.VMEM((2048, 256), jnp.bfloat16),
            pltpu.VMEM((16, 4, 128, 128), jnp.bfloat16),
            pltpu.VMEM((4, 640, 512), jnp.bfloat16),
            pltpu.VMEM((2048 // CHUNKS, 512), jnp.float32),
            pltpu.VMEM((32, 8, 16, 128), jnp.bfloat16),
            pltpu.VMEM((8, 2048), jnp.float32),
            pltpu.VMEM((8, 2048), jnp.float32),
            pltpu.VMEM((343, 2, 128), jnp.float32),
            pltpu.VMEM((7 * F1, 9, 2, 128), jnp.float32),
            pltpu.VMEM((NF, 9, 2, 128), jnp.float32),
            pltpu.VMEM((NF // 2, 9, 2, 8, 128), jnp.float32),
            pltpu.VMEM((189, 512), jnp.int32),
            pltpu.VMEM((4, 128), jnp.float32),
            pltpu.VMEM((16, 8, 128), jnp.float32),
            pltpu.VMEM((4, 128), jnp.int32),
            pltpu.SMEM((512,), jnp.int32),
            pltpu.SMEM((4, 16), jnp.int32),
            pltpu.VMEM((8, 2048), jnp.float32),
            pltpu.SMEM((512,), jnp.int32),
            pltpu.VMEM((256, 16, 128), jnp.bfloat16),
            pltpu.VMEM((512, 8, 128), jnp.float32),
            pltpu.VMEM((256, 8, 128), jnp.float32),
            pltpu.VMEM((512, 8, 128), jnp.float32),
            pltpu.VMEM((32 * F1, 8, 128), jnp.float32),
            pltpu.VMEM((NF, 4, 8, 128), jnp.float32),
            pltpu.VMEM((2, 32, 4, 16, 128), jnp.bfloat16),
            pltpu.SemaphoreType.DMA((11,)),
            pltpu.SemaphoreType.DMA((2, CHUNKS)),
            pltpu.SemaphoreType.DMA((2, CHUNKS)),
            pltpu.SemaphoreType.DMA,
            pltpu.SemaphoreType.DMA,
            pltpu.SemaphoreType.DMA,
            pltpu.SemaphoreType.DMA((2,)),
            pltpu.SemaphoreType.DMA((2,)),
            pltpu.SemaphoreType.DMA((2,)),
        ],
        compiler_params=pltpu.CompilerParams(collective_id=0, has_side_effects=True, vmem_limit_bytes=46 * 2**20),
    )(*[pltpu.with_memory_space_constraint(v, pltpu.HBM) for v in (child, interp, blocks, angle, slot_parent, far, trans)])


def arrange_kernel(src, dst, got, out, in_sem, out_sem):
    row = lax.broadcasted_iota(jnp.int32, (8, 128), 0)
    low, pick = row < 4, (row & 2) == 0

    def swap(a, b, mask, shift):
        return (
            jnp.where(mask, a, pltpu.roll(b, shift, 0)),
            jnp.where(mask, pltpu.roll(a, 8 - shift, 0), b),
        )

    fetch = [pltpu.make_async_copy(src.at[:, :, n], got.at[n], in_sem.at[n]) for n in range(4)]
    store = [pltpu.make_async_copy(out.at[pl.ds(4 * n, 4)], dst.at[pl.ds(4 * n, 4)], out_sem.at[n]) for n in range(4)]
    for copy in fetch:
        copy.start()
    for n in range(4):
        fetch[n].wait()
        for c in range(16):
            parts = [got[n, half, 2 * c + odd].astype(jnp.float32) for odd in range(2) for half in range(2)]
            lanes = slice(c * 128, c * 128 + 128)
            for k in range(2):
                v0, v1, v2, v3 = [v[8 * k : 8 * k + 8] for v in parts]
                p, r = swap(v0, v2, low, 4)
                q, s = swap(v1, v3, low, 4)
                at = 4 * n + 2 * k
                out[at, 0, :, lanes], out[at + 1, 0, :, lanes] = swap(p, q, pick, 2)
                out[at, 1, :, lanes], out[at + 1, 1, :, lanes] = swap(r, s, pick, 2)
        store[n].start()
    for copy in store:
        copy.wait()


def arrange(got):
    return pl.pallas_call(
        arrange_kernel,
        in_specs=[pl.BlockSpec(memory_space=pl.ANY)],
        out_specs=pl.BlockSpec(memory_space=pl.ANY),
        out_shape=jax.ShapeDtypeStruct((16, 2, 8, 2048), jnp.float32),
        scratch_shapes=[
            pltpu.VMEM((4, 2, 32, 16, 128), jnp.bfloat16),
            pltpu.VMEM((16, 2, 8, 2048), jnp.float32),
            pltpu.SemaphoreType.DMA((4,)),
            pltpu.SemaphoreType.DMA((4,)),
        ],
        compiler_params=pltpu.CompilerParams(vmem_limit_bytes=8 * 2**20),
    )(got)


def shards(child_pat, interp, interp_blocks, shift_angle, slot_parent, far_list, trans):
    pieces = far_pieces(
        child_pat.reshape(2048, 512),
        interp,
        interp_blocks.T,
        shift_angle,
        slot_parent,
        far_list.T,
        jnp.transpose(trans, (1, 0, 2)),
    )
    return arrange(pieces)


def solution(mesh):
    in_specs = (
        P("box", None, None, "dir"),
        P("dir", None, None, None),
        P("dir", None),
        P(None, "dir"),
        P(),
        P(),
        P(None, None, "dir"),
    )
    out_specs = P("box", None, None, "dir")
    return jax.shard_map(shards, mesh=mesh, in_specs=in_specs, out_specs=out_specs, check_vma=False)
```

profile of v0, /device:TPU:1, one launch (start us, length us, event | category | flops | bytes accessed | tf_op | source)
XLA Modules:
  0.0 65.3 jit_solution(9731359375569190784)
XLA Ops:
  0.0 63.7 %shard_map.73.src = bf16[2,32,4,16,128]{4,3,2,1,0:T(8,128)(2,1)S(1)} custom-call(bf16[2048,512]{1,0:T(8,128)(2,1)} %bitcast.5, bf16[16,4,128,128]{3,2,1,0:T(8,128)(2,1)} %interp.1, s32[4,16]{1,0:T(4,128)} %bitcast.7, f32[8,2048]{1,0:T(8,128)} %angle_in.1, s32[512]{0:T(512)} %slot_in.1, s32[189,512]{1,0:T(8,128)} %bitcast.6, f32[343,2,2048]{2,1,0:T(2,128)} %bitcast.4), custom_call_target="tpu_custom_call" | custom-call | tf_op jit(solution)/shard_map/pallas_call | solution.py:402
  63.7 1.6 %shard_map.74 = f32[16,2,8,2048]{3,2,1,0:T(8,128)} custom-call(bf16[2,32,4,16,128]{4,3,2,1,0:T(8,128)(2,1)S(1)} %shard_map.73.src), custom_call_target="tpu_custom_call" | custom-call | tf_op jit(solution)/shard_map/pallas_call | solution.py:482
where the time goes:
time: 65.4 us; the launch traced here: 65.3 us
  Pallas kernels  65.3 us (100%)
    pallas_call x1, Pallas kernels, far_pieces(): pl.pallas_call(main_kernel, in_specs=[any_space] * 7, out_specs=any_space...  63.7 us
    pallas_call x1, Pallas kernels, arrange(): pl.pallas_call(arrange_kernel, in_specs=[pl.BlockSpec(memory_space=pl.ANY...  1.62 us

commit v1 on v0

--- a/solution.py
+++ b/solution.py
@@ -68,7 +68,7 @@
 def main_kernel(
     child, interp, blocks_in, angle_in, slot_in, far, trans, out,
     own, before, after, weights, weight, total, stage, cosine, sine, raw, tab_z, tab, tiles,
-    listed, occ, mask, slot_vec, slot_of, blocks, angle, slot_parent,
+    listed, occ, mask, slot_vec, slot_of, slot_parent, blocks, angle,
     pats, wide_x, later, grid_x, lines, spec, back,
     load_sem, halo_send, halo_recv, move_send, move_recv, local_sem, home_sem, back_send, back_recv,
 ):
@@ -149,11 +149,11 @@
     zero = jnp.zeros((4, 128), jnp.int32)
     found = lax.fori_loop(0, 128, invert, (zero,) * 4, unroll=4)
     slot_vec[...] = jnp.maximum(jnp.maximum(found[0], found[1]), jnp.maximum(found[2], found[3]))
-    to_scalar = [
+    slot_copies = [
         pltpu.make_async_copy(slot_vec.at[t], slot_of.at[pl.ds(t * 128, 128)], load_sem.at[7 + t])
         for t in range(4)
     ]
-    for copy in to_scalar:
+    for copy in slot_copies:
         copy.start()
 
     loads[0].wait()
@@ -244,11 +244,17 @@
                 return carry
 
             lax.fori_loop(0, 4, tile_of, 0)
-        for peer in peers:
-            pltpu.make_async_remote_copy(
-                stage.at[peer, i], pats.at[bb * 8 + i], move_send, move_recv,
-                device_id={"box": peer},
-            ).start()
+            for core in range(2):
+                for z in range(4):
+                    peer = c * 8 + ((bb // 2 + 2 + z) % 4) * 2 + (bb + core) % 2
+
+                    @pl.when(peer != bb)
+                    def _(peer=peer):
+                        pltpu.make_async_remote_copy(
+                            stage.at[peer, i], pats.at[bb * 8 + i], move_send, move_recv,
+                            device_id={"box": peer},
+                        ).start()
+
         return carry
 
     lax.fori_loop(0, CHUNKS, chunk, 0)
@@ -272,7 +278,7 @@
         return lax.fori_loop(0, 9, inner, carry)
 
     lax.fori_loop(0, F1, expand, 0)
-    for copy in to_scalar:
+    for copy in slot_copies:
         copy.wait()
     mine.wait()
     pltpu.make_async_copy(pats.at[pl.ds(0, 248)], pats.at[pl.ds(0, 248)], move_recv).wait()
@@ -297,78 +303,74 @@
                     later[at] = jnp.where(pick, pltpu.roll(left, 6, 0), right)
                 else:
                     vals.append(later[at])
-            for f, v in enumerate(line_in(vals)):
-                lines[i * F1 + f] = v
+            vals = line_in(vals)
+            for fz in range(9):
+                left, right = vals[fz], vals[fz + 9]
+                lines[i * 9 + fz] = jnp.where(pick, left, pltpu.roll(right, 2, 0))
+                lines[(i + 32) * 9 + fz] = jnp.where(pick, pltpu.roll(left, 6, 0), right)
             return carry
 
         lax.fori_loop(0, 32, in_z, 0, unroll=4)
 
         def in_y(x, carry):
             def inner(fz, carry):
-                vals = line_in([lines[(x * 8 + y) * F1 + fz] for y in range(8)])
+                vals = line_in([lines[(x * 8 + y) * 9 + fz] for y in range(8)])
                 for fy, v in enumerate(vals):
-                    spec[fy * F1 + fz, x] = v
+                    spec[fy * 9 + fz, x] = v
                 return carry
 
-            return lax.fori_loop(0, F1, inner, carry, unroll=3)
-
-        lax.fori_loop(0, 4, in_y, 0)
-
-        def product(fy, carry):
-            def inner(fz, carry):
-                here, there = fy * F1 + fz, fy * F1 + fz + 9
-                src = [None] * 8
-                for x in range(4):
-                    left, right = spec[here, x], spec[there, x]
-                    src[x] = jnp.where(pick, left, pltpu.roll(right, 2, 0))
-                    src[x + 4] = jnp.where(pick, pltpu.roll(left, 6, 0), right)
-                turn = [pltpu.roll(v, 4, 0) for v in src]
-                sets = [
-                    ([src[2 * j] + src[2 * j + 1] for j in range(4)], [turn[2 * j] + turn[2 * j + 1] for j in range(4)]),
-                    (src[1::2], turn[1::2]),
-                    (src[0::2], turn[0::2]),
-                ]
-                sums = []
-                for g, (x, t) in enumerate(sets):
-                    acc = [None] * 4
-                    for j in range(-1, 2):
-                        a = tiles[fy * 9 + fz, g * 3 + j + 1, 0]
-                        b = tiles[fy * 9 + fz, g * 3 + j + 1, 1]
-                        for i in range(4):
-                            if 0 <= i + j < 4:
-                                v = a * x[i + j] + b * t[i + j]
-                                acc[i] = v if acc[i] is None else acc[i] + v
-                    sums.append(acc)
-                res = []
-                for i in range(4):
-                    res += [sums[0][i] + sums[1][i], sums[0][i] + sums[2][i]]
-                for x in range(4):
-                    spec[here, x] = jnp.where(pick, res[x], pltpu.roll(res[x + 4], 2, 0))
-                    spec[there, x] = jnp.where(pick, pltpu.roll(res[x], 6, 0), res[x + 4])
-                return carry
-
-            return lax.fori_loop(0, 9, inner, carry, unroll=9)
-
-        lax.fori_loop(0, F1, product, 0)
+            return lax.fori_loop(0, 9, inner, carry, unroll=3)
+
+        lax.fori_loop(0, 8, in_y, 0)
+
+        def product(f, carry):
+            src = [spec[f, x] for x in range(8)]
+            turn = [pltpu.roll(v, 4, 0) for v in src]
+            sets = [
+                ([src[2 * j] + src[2 * j + 1] for j in range(4)], [turn[2 * j] + turn[2 * j + 1] for j in range(4)]),
+                (src[1::2], turn[1::2]),
+                (src[0::2], turn[0::2]),
+            ]
+            sums = []
+            for g, (x, t) in enumerate(sets):
+                acc = [None] * 4
+                for j in range(-1, 2):
+                    a, b = tiles[f, g * 3 + j + 1, 0], tiles[f, g * 3 + j + 1, 1]
+                    for i in range(4):
+                        if 0 <= i + j < 4:
+                            v = a * x[i + j] + b * t[i + j]
+                            acc[i] = v if acc[i] is None else acc[i] + v
+                sums.append(acc)
+            for i in range(4):
+                spec[f, 2 * i] = sums[0][i] + sums[1][i]
+                spec[f, 2 * i + 1] = sums[0][i] + sums[2][i]
+            return carry
+
+        lax.fori_loop(0, NF // 2, product, 0, unroll=9)
 
         def out_y(x, carry):
             def inner(fz, carry):
-                vals = line_out([spec[fy * F1 + fz, x] for fy in range(F1)])
+                vals = line_out([spec[fy * 9 + fz, x] for fy in range(F1)])
                 for y, v in enumerate(vals):
-                    lines[(x * 8 + y) * F1 + fz] = v
+                    lines[(x * 8 + y) * 9 + fz] = v
                 return carry
 
-            return lax.fori_loop(0, F1, inner, carry, unroll=3)
-
-        lax.fori_loop(0, 4, out_y, 0)
+            return lax.fori_loop(0, 9, inner, carry, unroll=3)
+
+        lax.fori_loop(0, 8, out_y, 0)
 
         def out_z(i, carry):
-            for z, v in enumerate(line_out([lines[i * F1 + f] for f in range(F1)])):
+            near, away = [], []
+            for fz in range(9):
+                left, right = lines[i * 9 + fz], lines[(i + 32) * 9 + fz]
+                near.append(jnp.where(pick, left, pltpu.roll(right, 2, 0)))
+                away.append(jnp.where(pick, pltpu.roll(left, 6, 0), right))
+            for z, v in enumerate(line_out(near + away)):
                 grid_x[i * 8 + z] = v
                 grid_x[256 + i * 8 + z] = pltpu.roll(v, 6, 0)
             return carry
 
-        lax.fori_loop(0, 32, out_z, 0, unroll=4)
+        lax.fori_loop(0, 32, out_z, 0, unroll=2)
 
         def give(target, half=half):
             for q in range(4):
@@ -423,15 +425,15 @@
             pltpu.VMEM((16, 8, 128), jnp.float32),
             pltpu.VMEM((4, 128), jnp.int32),
             pltpu.SMEM((512,), jnp.int32),
+            pltpu.SMEM((512,), jnp.int32),
             pltpu.SMEM((4, 16), jnp.int32),
             pltpu.VMEM((8, 2048), jnp.float32),
-            pltpu.SMEM((512,), jnp.int32),
             pltpu.VMEM((256, 16, 128), jnp.bfloat16),
             pltpu.VMEM((512, 8, 128), jnp.float32),
             pltpu.VMEM((256, 8, 128), jnp.float32),
             pltpu.VMEM((512, 8, 128), jnp.float32),
             pltpu.VMEM((32 * F1, 8, 128), jnp.float32),
-            pltpu.VMEM((NF, 4, 8, 128), jnp.float32),
+            pltpu.VMEM((NF // 2, 8, 8, 128), jnp.float32),
             pltpu.VMEM((2, 32, 4, 16, 128), jnp.bfloat16),
             pltpu.SemaphoreType.DMA((11,)),
             pltpu.SemaphoreType.DMA((2, CHUNKS)),

time: 65.4 us -> 64.5 us (0.986)
  Pallas kernels: 65.3 us -> 64.4 us
    pallas_call x1, Pallas kernels: 63.7 us -> 62.8 us  [far_pieces(): pl.pallas_call(main_kernel, in_specs=[any_space] * 7, out_specs=any_space...]
where the time goes in v1:
time: 64.5 us; the launch traced here: 64.4 us
  Pallas kernels  64.4 us (100%)
    pallas_call x1, Pallas kernels, far_pieces(): pl.pallas_call(main_kernel, in_specs=[any_space] * 7, out_specs=any_space...  62.8 us
    pallas_call x1, Pallas kernels, arrange(): pl.pallas_call(arrange_kernel, in_specs=[pl.BlockSpec(memory_space=pl.ANY...  1.62 us

profile of v1, /device:TPU:1, one launch (start us, length us, event | category | flops | bytes accessed | tf_op | source)
XLA Modules:
  0.0 64.4 jit_solution(6237204791699350777)
XLA Ops:
  0.0 62.8 %shard_map.73.src = bf16[2,32,4,16,128]{4,3,2,1,0:T(8,128)(2,1)S(1)} custom-call(bf16[2048,512]{1,0:T(8,128)(2,1)} %bitcast.5, bf16[16,4,128,128]{3,2,1,0:T(8,128)(2,1)} %interp.1, s32[4,16]{1,0:T(4,128)} %bitcast.7, f32[8,2048]{1,0:T(8,128)} %angle_in.1, s32[512]{0:T(512)} %slot_in.1, s32[189,512]{1,0:T(8,128)} %bitcast.6, f32[343,2,2048]{2,1,0:T(2,128)} %bitcast.4), custom_call_target="tpu_custom_call" | custom-call | tf_op jit(solution)/shard_map/pallas_call | solution.py:404
  62.8 1.6 %shard_map.74 = f32[16,2,8,2048]{3,2,1,0:T(8,128)} custom-call(bf16[2,32,4,16,128]{4,3,2,1,0:T(8,128)(2,1)S(1)} %shard_map.73.src), custom_call_target="tpu_custom_call" | custom-call | tf_op jit(solution)/shard_map/pallas_call | solution.py:484

commit v2 on v1

--- a/solution.py
+++ b/solution.py
@@ -55,8 +55,8 @@
     return out
 
 
-TURNS = [(1, 1), (3, 1), (3, 3), (1, 3), (2, 2), (1, 2), (2, 1), (3, 2), (2, 3), (1, 0), (0, 1), (3, 0), (0, 3), (2, 0), (0, 2)]
-PEERS = [(0, 0, 1)] + [(x, z, c) for c in range(2) for x, z in TURNS]
+TURNS = [(2, 2), (1, 2), (2, 1), (3, 2), (2, 3), (1, 1), (3, 1), (3, 3), (1, 3), (2, 0), (0, 2), (1, 0), (0, 1), (3, 0), (0, 3)]
+PEERS = [(x, z, c) for x, z in TURNS for c in range(2)] + [(0, 0, 1)]
 CHUNKS = 8
 
 
@@ -217,18 +217,18 @@
                     preferred_element_type=jnp.float32,
                 )
                 acc = piece if acc is None else acc + piece
-            total[...] = acc
+            total[c % 2] = acc
 
             def tile_of(tile, carry, c=c):
-                lane = pl.multiple_of(tile * 128, 128)
-                wide = pl.multiple_of(c * 512 + tile * 128, 128)
+                lane = tile * 128
+                wide = c * 512 + tile * 128
                 halves = [[], []]
                 for k in range(2):
                     re = im = None
                     for h in range(8):
                         base = k * 128 + h * 16
-                        ur = total[pl.ds(base, 8), pl.ds(lane, 128)]
-                        ui = total[pl.ds(base + 8, 8), pl.ds(lane, 128)]
+                        ur = total[c % 2, pl.ds(base, 8), pl.ds(lane, 128)]
+                        ui = total[c % 2, pl.ds(base + 8, 8), pl.ds(lane, 128)]
                         cs = jnp.broadcast_to(cosine[h : h + 1, pl.ds(wide, 128)], (8, 128))
                         sn = jnp.broadcast_to(sine[h : h + 1, pl.ds(wide, 128)], (8, 128))
                         r, m = cs * ur - sn * ui, sn * ur + cs * ui
@@ -243,18 +243,13 @@
                     stage[(c * 4 + tile) * 2 + k, i] = value
                 return carry
 
-            lax.fori_loop(0, 4, tile_of, 0)
-            for core in range(2):
-                for z in range(4):
-                    peer = c * 8 + ((bb // 2 + 2 + z) % 4) * 2 + (bb + core) % 2
-
-                    @pl.when(peer != bb)
-                    def _(peer=peer):
-                        pltpu.make_async_remote_copy(
-                            stage.at[peer, i], pats.at[bb * 8 + i], move_send, move_recv,
-                            device_id={"box": peer},
-                        ).start()
-
+            for tile in range(4):
+                tile_of(tile, 0)
+        for peer in peers:
+            pltpu.make_async_remote_copy(
+                stage.at[peer, i], pats.at[bb * 8 + i], move_send, move_recv,
+                device_id={"box": peer},
+            ).start()
         return carry
 
     lax.fori_loop(0, CHUNKS, chunk, 0)
@@ -310,7 +305,7 @@
                 lines[(i + 32) * 9 + fz] = jnp.where(pick, pltpu.roll(left, 6, 0), right)
             return carry
 
-        lax.fori_loop(0, 32, in_z, 0, unroll=4)
+        lax.fori_loop(0, 32, in_z, 0, unroll=8)
 
         def in_y(x, carry):
             def inner(fz, carry):
@@ -319,7 +314,7 @@
                     spec[fy * 9 + fz, x] = v
                 return carry
 
-            return lax.fori_loop(0, 9, inner, carry, unroll=3)
+            return lax.fori_loop(0, 9, inner, carry, unroll=9)
 
         lax.fori_loop(0, 8, in_y, 0)
 
@@ -346,7 +341,7 @@
                 spec[f, 2 * i + 1] = sums[0][i] + sums[2][i]
             return carry
 
-        lax.fori_loop(0, NF // 2, product, 0, unroll=9)
+        lax.fori_loop(0, NF // 2, product, 0, unroll=18)
 
         def out_y(x, carry):
             def inner(fz, carry):
@@ -355,7 +350,7 @@
                     lines[(x * 8 + y) * 9 + fz] = v
                 return carry
 
-            return lax.fori_loop(0, 9, inner, carry, unroll=3)
+            return lax.fori_loop(0, 9, inner, carry, unroll=9)
 
         lax.fori_loop(0, 8, out_y, 0)
 
@@ -370,7 +365,7 @@
                 grid_x[256 + i * 8 + z] = pltpu.roll(v, 6, 0)
             return carry
 
-        lax.fori_loop(0, 32, out_z, 0, unroll=2)
+        lax.fori_loop(0, 32, out_z, 0, unroll=8)
 
         def give(target, half=half):
             for q in range(4):
@@ -412,7 +407,7 @@
             pltpu.VMEM((2048, 256), jnp.bfloat16),
             pltpu.VMEM((16, 4, 128, 128), jnp.bfloat16),
             pltpu.VMEM((4, 640, 512), jnp.bfloat16),
-            pltpu.VMEM((2048 // CHUNKS, 512), jnp.float32),
+            pltpu.VMEM((2, 2048 // CHUNKS, 512), jnp.float32),
             pltpu.VMEM((32, 8, 16, 128), jnp.bfloat16),
             pltpu.VMEM((8, 2048), jnp.float32),
             pltpu.VMEM((8, 2048), jnp.float32),

time: 64.5 us -> 61.8 us (0.958)
  Pallas kernels: 64.4 us -> 61.7 us
    pallas_call x1, Pallas kernels: 62.8 us -> 60.1 us  [far_pieces(): pl.pallas_call(main_kernel, in_specs=[any_space] * 7, out_specs=any_space...]
where the time goes in v2:
time: 61.8 us; the launch traced here: 61.7 us
  Pallas kernels  61.7 us (100%)
    pallas_call x1, Pallas kernels, far_pieces(): pl.pallas_call(main_kernel, in_specs=[any_space] * 7, out_specs=any_space...  60.1 us
    pallas_call x1, Pallas kernels, arrange(): pl.pallas_call(arrange_kernel, in_specs=[pl.BlockSpec(memory_space=pl.ANY...  1.62 us

profile of v2, /device:TPU:1, one launch (start us, length us, event | category | flops | bytes accessed | tf_op | source)
XLA Modules:
  0.0 61.7 jit_solution(15264750254336076317)
XLA Ops:
  0.0 60.1 %shard_map.73.src = bf16[2,32,4,16,128]{4,3,2,1,0:T(8,128)(2,1)S(1)} custom-call(bf16[2048,512]{1,0:T(8,128)(2,1)} %bitcast.5, bf16[16,4,128,128]{3,2,1,0:T(8,128)(2,1)} %interp.1, s32[4,16]{1,0:T(4,128)} %bitcast.7, f32[8,2048]{1,0:T(8,128)} %angle_in.1, s32[512]{0:T(512)} %slot_in.1, s32[189,512]{1,0:T(8,128)} %bitcast.6, f32[343,2,2048]{2,1,0:T(2,128)} %bitcast.4), custom_call_target="tpu_custom_call" | custom-call | tf_op jit(solution)/shard_map/pallas_call | solution.py:399
  60.1 1.6 %shard_map.74 = f32[16,2,8,2048]{3,2,1,0:T(8,128)} custom-call(bf16[2,32,4,16,128]{4,3,2,1,0:T(8,128)(2,1)S(1)} %shard_map.73.src), custom_call_target="tpu_custom_call" | custom-call | tf_op jit(solution)/shard_map/pallas_call | solution.py:479

commit v3 on v2

--- a/solution.py
+++ b/solution.py
@@ -57,7 +57,7 @@
 
 TURNS = [(2, 2), (1, 2), (2, 1), (3, 2), (2, 3), (1, 1), (3, 1), (3, 3), (1, 3), (2, 0), (0, 2), (1, 0), (0, 1), (3, 0), (0, 3)]
 PEERS = [(x, z, c) for x, z in TURNS for c in range(2)] + [(0, 0, 1)]
-CHUNKS = 8
+CHUNKS = 16
 
 
 def peers_of(bb):
@@ -69,7 +69,7 @@
     child, interp, blocks_in, angle_in, slot_in, far, trans, out,
     own, before, after, weights, weight, total, stage, cosine, sine, raw, tab_z, tab, tiles,
     listed, occ, mask, slot_vec, slot_of, slot_parent, blocks, angle,
-    pats, wide_x, later, grid_x, lines, spec, back,
+    pats, later, grid_x, lines, spec, back,
     load_sem, halo_send, halo_recv, move_send, move_recv, local_sem, home_sem, back_send, back_recv,
 ):
     bb, dd = lax.axis_index("box"), lax.axis_index("dir")
@@ -222,38 +222,32 @@
             def tile_of(tile, carry, c=c):
                 lane = tile * 128
                 wide = c * 512 + tile * 128
-                halves = [[], []]
-                for k in range(2):
-                    re = im = None
-                    for h in range(8):
-                        base = k * 128 + h * 16
-                        ur = total[c % 2, pl.ds(base, 8), pl.ds(lane, 128)]
-                        ui = total[c % 2, pl.ds(base + 8, 8), pl.ds(lane, 128)]
-                        cs = jnp.broadcast_to(cosine[h : h + 1, pl.ds(wide, 128)], (8, 128))
-                        sn = jnp.broadcast_to(sine[h : h + 1, pl.ds(wide, 128)], (8, 128))
-                        r, m = cs * ur - sn * ui, sn * ur + cs * ui
-                        re = r if re is None else re + r
-                        im = m if im is None else im + m
-                    keep = mask[2 * i + k]
-                    re, im = re * keep, im * keep
-                    halves[0].append(jnp.where(low, re, pltpu.roll(im, 4, 0)))
-                    halves[1].append(jnp.where(low, pltpu.roll(re, 4, 0), im))
-                for k in range(2):
-                    value = jnp.concatenate(halves[k], axis=0).astype(jnp.bfloat16)
-                    stage[(c * 4 + tile) * 2 + k, i] = value
+                re = im = None
+                for h in range(8):
+                    ur = total[c % 2, pl.ds(h * 16, 8), pl.ds(lane, 128)]
+                    ui = total[c % 2, pl.ds(h * 16 + 8, 8), pl.ds(lane, 128)]
+                    cs = jnp.broadcast_to(cosine[h : h + 1, pl.ds(wide, 128)], (8, 128))
+                    sn = jnp.broadcast_to(sine[h : h + 1, pl.ds(wide, 128)], (8, 128))
+                    r, m = cs * ur - sn * ui, sn * ur + cs * ui
+                    re = r if re is None else re + r
+                    im = m if im is None else im + m
+                keep = mask[i]
+                re, im = re * keep, im * keep
+                stage[(c * 4 + tile) * 2, i] = jnp.where(low, re, pltpu.roll(im, 4, 0)).astype(jnp.bfloat16)
+                stage[(c * 4 + tile) * 2 + 1, i] = jnp.where(low, pltpu.roll(re, 4, 0), im).astype(jnp.bfloat16)
                 return carry
 
             for tile in range(4):
                 tile_of(tile, 0)
         for peer in peers:
             pltpu.make_async_remote_copy(
-                stage.at[peer, i], pats.at[bb * 8 + i], move_send, move_recv,
+                stage.at[peer, i], pats.at[bb * 16 + i], move_send, move_recv,
                 device_id={"box": peer},
             ).start()
         return carry
 
     lax.fori_loop(0, CHUNKS, chunk, 0)
-    mine = pltpu.make_async_copy(stage.at[bb], pats.at[pl.ds(bb * 8, 8)], local_sem)
+    mine = pltpu.make_async_copy(stage.at[bb], pats.at[pl.ds(bb * 16, 16)], local_sem)
     mine.start()
     pick = (row & 2) == 0
 
@@ -276,15 +270,7 @@
     for copy in slot_copies:
         copy.wait()
     mine.wait()
-    pltpu.make_async_copy(pats.at[pl.ds(0, 248)], pats.at[pl.ds(0, 248)], move_recv).wait()
-
-    def widen(i, carry):
-        both = pats[i].astype(jnp.float32)
-        wide_x[2 * i] = both[0:8]
-        wide_x[2 * i + 1] = both[8:16]
-        return carry
-
-    lax.fori_loop(0, 256, widen, 0, unroll=8)
+    pltpu.make_async_copy(pats.at[pl.ds(0, 496)], pats.at[pl.ds(0, 496)], move_recv).wait()
 
     for half in range(2):
 
@@ -293,7 +279,7 @@
             for z in range(8):
                 at = i * 8 + z
                 if half == 0:
-                    left, right = wide_x[slot_of[at]], wide_x[slot_of[at + 256]]
+                    left, right = pats[slot_of[at]].astype(jnp.float32), pats[slot_of[at + 256]].astype(jnp.float32)
                     vals.append(jnp.where(pick, left, pltpu.roll(right, 2, 0)))
                     later[at] = jnp.where(pick, pltpu.roll(left, 6, 0), right)
                 else:
@@ -408,7 +394,7 @@
             pltpu.VMEM((16, 4, 128, 128), jnp.bfloat16),
             pltpu.VMEM((4, 640, 512), jnp.bfloat16),
             pltpu.VMEM((2, 2048 // CHUNKS, 512), jnp.float32),
-            pltpu.VMEM((32, 8, 16, 128), jnp.bfloat16),
+            pltpu.VMEM((32, 16, 8, 128), jnp.bfloat16),
             pltpu.VMEM((8, 2048), jnp.float32),
             pltpu.VMEM((8, 2048), jnp.float32),
             pltpu.VMEM((343, 2, 128), jnp.float32),
@@ -423,8 +409,7 @@
             pltpu.SMEM((512,), jnp.int32),
             pltpu.SMEM((4, 16), jnp.int32),
             pltpu.VMEM((8, 2048), jnp.float32),
-            pltpu.VMEM((256, 16, 128), jnp.bfloat16),
-            pltpu.VMEM((512, 8, 128), jnp.float32),
+            pltpu.VMEM((512, 8, 128), jnp.bfloat16),
             pltpu.VMEM((256, 8, 128), jnp.float32),
             pltpu.VMEM((512, 8, 128), jnp.float32),
             pltpu.VMEM((32 * F1, 8, 128), jnp.float32),

time: 61.8 us -> 61.4 us (level)
  no operation moved by 1% of the time
where the time goes in v3:
time: 61.4 us; the launch traced here: 61.3 us
  Pallas kernels  61.3 us (100%)
    pallas_call x1, Pallas kernels, far_pieces(): pl.pallas_call(main_kernel, in_specs=[any_space] * 7, out_specs=any_space...  59.7 us
    pallas_call x1, Pallas kernels, arrange(): pl.pallas_call(arrange_kernel, in_specs=[pl.BlockSpec(memory_space=pl.ANY...  1.62 us

profile of v3, /device:TPU:1, one launch (start us, length us, event | category | flops | bytes accessed | tf_op | source)
XLA Modules:
  0.0 61.3 jit_solution(2381082272465211739)
XLA Ops:
  0.0 59.7 %shard_map.73.src = bf16[2,32,4,16,128]{4,3,2,1,0:T(8,128)(2,1)S(1)} custom-call(bf16[2048,512]{1,0:T(8,128)(2,1)} %bitcast.5, bf16[16,4,128,128]{3,2,1,0:T(8,128)(2,1)} %interp.1, s32[4,16]{1,0:T(4,128)} %bitcast.7, f32[8,2048]{1,0:T(8,128)} %angle_in.1, s32[512]{0:T(512)} %slot_in.1, s32[189,512]{1,0:T(8,128)} %bitcast.6, f32[343,2,2048]{2,1,0:T(2,128)} %bitcast.4), custom_call_target="tpu_custom_call" | custom-call | tf_op jit(solution)/shard_map/pallas_call | solution.py:385
  59.7 1.6 %shard_map.74 = f32[16,2,8,2048]{3,2,1,0:T(8,128)} custom-call(bf16[2,32,4,16,128]{4,3,2,1,0:T(8,128)(2,1)S(1)} %shard_map.73.src), custom_call_target="tpu_custom_call" | custom-call | tf_op jit(solution)/shard_map/pallas_call | solution.py:464

commit v4 on v3

--- a/solution.py
+++ b/solution.py
@@ -92,8 +92,6 @@
         pltpu.make_async_copy(slot_in, slot_parent, load_sem.at[5]),
         pltpu.make_async_copy(angle_in, angle, load_sem.at[6]),
     ]
-    for copy in loads:
-        copy.start()
     pl.semaphore_wait(barrier, len(peers) + 2)
 
     def halo(i):
@@ -112,6 +110,8 @@
     for i in range(CHUNKS):
         for copy in halo(i):
             copy.start()
+    for copy in loads:
+        copy.start()
 
     loads[6].wait()
     cosine[...] = jnp.cos(angle[...])

time: 61.4 us -> 61.4 us (level)
  no operation moved by 1% of the time
where the time goes in v4:
time: 61.4 us; the launch traced here: 61.3 us
  Pallas kernels  61.3 us (100%)
    pallas_call x1, Pallas kernels, far_pieces(): pl.pallas_call(main_kernel, in_specs=[any_space] * 7, out_specs=any_space...  59.7 us
    pallas_call x1, Pallas kernels, arrange(): pl.pallas_call(arrange_kernel, in_specs=[pl.BlockSpec(memory_space=pl.ANY...  1.62 us

profile of v4, /device:TPU:1, one launch (start us, length us, event | category | flops | bytes accessed | tf_op | source)
XLA Modules:
  0.0 61.3 jit_solution(1037551457333968638)
XLA Ops:
  0.0 59.7 %shard_map.73.src = bf16[2,32,4,16,128]{4,3,2,1,0:T(8,128)(2,1)S(1)} custom-call(bf16[2048,512]{1,0:T(8,128)(2,1)} %bitcast.5, bf16[16,4,128,128]{3,2,1,0:T(8,128)(2,1)} %interp.1, s32[4,16]{1,0:T(4,128)} %bitcast.7, f32[8,2048]{1,0:T(8,128)} %angle_in.1, s32[512]{0:T(512)} %slot_in.1, s32[189,512]{1,0:T(8,128)} %bitcast.6, f32[343,2,2048]{2,1,0:T(2,128)} %bitcast.4), custom_call_target="tpu_custom_call" | custom-call | tf_op jit(solution)/shard_map/pallas_call | solution.py:385
  59.7 1.6 %shard_map.74 = f32[16,2,8,2048]{3,2,1,0:T(8,128)} custom-call(bf16[2,32,4,16,128]{4,3,2,1,0:T(8,128)(2,1)S(1)} %shard_map.73.src), custom_call_target="tpu_custom_call" | custom-call | tf_op jit(solution)/shard_map/pallas_call | solution.py:464
